TPU v7x, 256 devices: a whole 4x4x8 slice. The times are simulated.
256 devices in a mesh: pool: 32 (over y, z), head: 8 (over x, core).
Axes of the slice: x: 4, y: 4, z: 8, core: 2. Of those that a mesh axis runs over, the one named last changes fastest.
Arguments:
- queries: bfloat16 [32, 256, 8192], P('pool', None, 'head'), may hold values from -6 to 6
- new_kv: bfloat16 [32, 256, 2048], P('pool', None, 'head'), may hold values from -6 to 6
- pool: bfloat16 [1024, 256, 2048], P('pool', None, 'head'), may hold values from -6 to 6
- page_owner: int32 [32, 32], replicated, may hold values from 0 to 31, as said below
- page_slot: int32 [32, 32], replicated, may hold values from 0 to 31, as said below
- cached_len: int32 [32], replicated, may hold values from 1 to 8192, as said below
Outputs:
- attended: bfloat16 [32, 256, 8192], P('pool', None, 'head')
Inputs may be any that keep to these rules, and one draw needn't show every extreme that they name: `page_owner`: each of the 32 entries of a row is the owner of that page of the request; every owner holds exactly 1 entries of each row. Pairs (page_owner, page_slot) are distinct over all requests and pages. Request r uses its first ceil(cached_len[r] / 256) pages; some request has exactly 8192 cached tokens.
All inputs are finite; a program needn't handle non-finite values.
Results may differ from a plain program's by a relative error of at most 0.0075.
Values may be sent and summed in bfloat16 or wider, within the bound.
No kernel may reach another device: no remote copies, remote signals or barrier semaphores. Data moves between devices by JAX's collectives and lax.ppermute only.
A program may use at most 64 MiB of HBM per device.

v0:
```python
import math

import jax
import jax.numpy as jnp
from jax import lax
from jax.experimental import pallas as pl
from jax.experimental.pallas import tpu as pltpu
from jax.sharding import PartitionSpec as P


HD = 128
PAGE = 256
NY = 4
NZ = 8
SCALE = math.log2(math.e) / math.sqrt(HD)
MASKED = -1e30


def gather_pages(pool, slots, base, counts):
    def body(slot_ref, pool_ref, *outs):
        places = [(out, i) for out, count in zip(outs, counts) for i in range(count)]
        for k, (out, i) in enumerate(places):
            out[i] = pool_ref[slot_ref[base + k]]

    whole = pl.BlockSpec(memory_space=pltpu.VMEM)
    return pl.pallas_call(
        body,
        in_specs=[pl.BlockSpec(memory_space=pltpu.SMEM), whole],
        out_specs=[whole] * len(counts),
        out_shape=[jax.ShapeDtypeStruct((c,) + pool.shape[1:], pool.dtype) for c in counts],
        compiler_params=pltpu.CompilerParams(vmem_limit_bytes=4 << 20),
    )(slots, pool)


def bundles(arrays, plans):
    plans = [
        [(i, p[0]) for i in range(len(arrays))] if len(p) == 1 else list(p) for p in plans
    ]

    def body(*refs):
        ins, outs = refs[: len(arrays)], refs[len(arrays) :]
        for out, plan in zip(outs, plans):
            for at, (i, k) in enumerate(plan):
                out[at] = ins[i][k]

    whole = pl.BlockSpec(memory_space=pltpu.VMEM)
    return pl.pallas_call(
        body,
        in_specs=[whole] * len(arrays),
        out_specs=[whole] * len(plans),
        out_shape=[
            jax.ShapeDtypeStruct((len(p),) + arrays[0].shape[1:], arrays[0].dtype) for p in plans
        ],
        compiler_params=pltpu.CompilerParams(vmem_limit_bytes=4 << 20),
    )(*arrays)


def attend(q, state, lims, base, pieces, fresh, mode, unroll=8):
    heads = q.shape[1] // HD
    rows = q.shape[0]
    npg = sum(len(ids) for _, ids in pieces)
    lead = 1 if fresh is not None else 0
    nkv = npg + lead
    has_state = state is not None

    def body(lim_ref, q_ref, *refs):
        refs = list(refs)
        st_in = refs.pop(0) if has_state else None
        fr = refs.pop(0) if lead else None
        pgs = [refs.pop(0) for _ in pieces]
        out = refs.pop(0)
        k_ref, v_ref, stat_ref = refs
        v_ref[:, HD:] = jnp.ones((nkv * PAGE, HD), jnp.bfloat16)
        blocks = [fr[...]] if lead else []
        for pg, (_, ids) in zip(pgs, pieces):
            blocks += [pg[i] for i in ids]
        for i, blk in enumerate(blocks):
            at = i * PAGE
            k_ref[at : at + PAGE] = blk[:, :HD]
            v_ref[at : at + PAGE, :HD] = blk[:, HD:]
        lane = lax.broadcasted_iota(jnp.int32, (1, PAGE), 1)
        bias = [jnp.where(lane < lim_ref[base + i], 0.0, MASKED) for i in range(npg)]
        lanes = lax.broadcasted_iota(jnp.int32, (rows, HD), 1)
        if mode != "state":
            stat_ref[...] = jnp.zeros((rows, HD), jnp.float32)

        def one_head(h):
            at = pl.multiple_of(h * HD, HD)
            qh = q_ref[:, pl.ds(at, HD)]
            s = lax.dot_general(
                qh, k_ref[...], (((1,), (1,)), ((), ())), preferred_element_type=jnp.float32
            )
            cols = []
            for i in range(nkv):
                c = s[:, i * PAGE : (i + 1) * PAGE] * SCALE
                if i < lead:
                    r_i = lax.broadcasted_iota(jnp.int32, (rows, PAGE), 0)
                    c_i = lax.broadcasted_iota(jnp.int32, (rows, PAGE), 1)
                    c = jnp.where(c_i <= r_i, c, MASKED)
                else:
                    c = c + bias[i - lead]
                cols.append(c)
            s = jnp.concatenate(cols, axis=1) if nkv > 1 else cols[0]
            peak = jnp.max(s, axis=-1, keepdims=True)
            if has_state:
                old = st_in[h]
                old_peak = old[:, 2 * HD - 1 :]
                peak = jnp.maximum(peak, old_peak)
                shrink = jnp.exp2(old_peak - peak)
            w = jnp.exp2(s - peak).astype(jnp.bfloat16)
            acc = jnp.dot(w, v_ref[...], preferred_element_type=jnp.float32)
            if has_state:
                acc = acc + old * shrink
            if mode == "state":
                out[h, :, :HD] = acc[:, :HD]
                out[h, :, HD:] = jnp.where(lanes < HD // 2, acc[:, HD:], peak)
            else:
                total = acc[:, HD:]
                if has_state:
                    total = jnp.where(lanes < HD // 2, total, pltpu.roll(total, HD // 2, 1))
                out[:, pl.ds(at, HD)] = (acc[:, :HD] / total).astype(out.dtype)
                lse = peak + jnp.log2(total)
                stat = stat_ref[...]
                if mode == "home":
                    stat = jnp.where(lanes == h, lse, stat)
                else:
                    hi = lse.astype(jnp.bfloat16).astype(jnp.float32)
                    mid = (lse - hi).astype(jnp.bfloat16).astype(jnp.float32)
                    for part, off in ((hi, 0), (mid, heads), (lse - hi - mid, 2 * heads)):
                        stat = jnp.where(lanes == h + off, part, stat)
                stat_ref[...] = stat

        def some_heads(g, carry):
            for u in range(unroll):
                one_head(g * unroll + u)
            return carry

        lax.fori_loop(0, heads // unroll, some_heads, 0)
        if mode != "state":
            out[:, heads * HD :] = stat_ref[...].astype(out.dtype)

    args = [q]
    if has_state:
        args.append(state)
    if lead:
        args.append(fresh)
    args += [arr for arr, _ in pieces]
    whole = pl.BlockSpec(memory_space=pltpu.VMEM)
    if mode != "state":
        kind = jnp.float32 if mode == "home" else jnp.bfloat16
        out_shape = jax.ShapeDtypeStruct((rows, (heads + 1) * HD), kind)
    else:
        out_shape = jax.ShapeDtypeStruct((heads, rows, 2 * HD), jnp.float32)
    return pl.pallas_call(
        body,
        in_specs=[pl.BlockSpec(memory_space=pltpu.SMEM)] + [whole] * len(args),
        out_specs=whole,
        scratch_shapes=[
            pltpu.VMEM((nkv * PAGE, HD), jnp.bfloat16),
            pltpu.VMEM((nkv * PAGE, 2 * HD), jnp.bfloat16),
            pltpu.VMEM((rows, HD), jnp.float32),
        ],
        out_shape=out_shape,
        input_output_aliases={2: 0} if has_state and mode == "state" else {},
        compiler_params=pltpu.CompilerParams(vmem_limit_bytes=16 << 20),
    )(lims, *args)


def merge(home, parts):
    rows = home.shape[0]
    heads = home.shape[1] // HD - 1

    def body(home_ref, *refs):
        part_refs, out = refs[:-1], refs[-1]
        lses = [home_ref[:, heads * HD :]]
        for p in part_refs:
            st = p[:, heads * HD :].astype(jnp.float32)
            lses.append(
                st + pltpu.roll(st, HD - heads, 1) + pltpu.roll(st, HD - 2 * heads, 1)
            )
        top = lses[0]
        for lse in lses[1:]:
            top = jnp.maximum(top, lse)
        ws = [jnp.exp2(lse - top) for lse in lses]
        total = ws[0]
        for w in ws[1:]:
            total = total + w
        ws = [w / total for w in ws]
        for h in range(heads):
            cut = slice(h * HD, (h + 1) * HD)
            acc = home_ref[:, cut] * ws[0][:, h : h + 1]
            for p, w in zip(part_refs, ws[1:]):
                acc = acc + p[:, cut].astype(jnp.float32) * w[:, h : h + 1]
            out[:, cut] = acc.astype(jnp.bfloat16)

    whole = pl.BlockSpec(memory_space=pltpu.VMEM)
    return pl.pallas_call(
        body,
        in_specs=[whole] * (1 + len(parts)),
        out_specs=whole,
        out_shape=jax.ShapeDtypeStruct((rows, heads * HD), jnp.bfloat16),
        compiler_params=pltpu.CompilerParams(vmem_limit_bytes=16 << 20),
    )(home, *parts)


def shift(x, dy, dz):
    pairs = [
        (s, ((s // NZ + dy) % NY) * NZ + (s % NZ + dz) % NZ) for s in range(NY * NZ)
    ]
    return lax.ppermute(x, "pool", pairs)


ROWS = (1, 3, 2)


def on_device(queries, new_kv, pool, page_owner, page_slot, cached_len):
    me = lax.axis_index("pool")
    y = me >> 3
    z = me & (NZ - 1)
    q = queries[0]
    i32 = jnp.int32

    q_up = shift(q, 0, 1)

    goal = [(dy, -4) for dy in range(NY)] + [(dy, 3) for dy in range(NY)]
    goal += [(dy, e) for dy in ROWS for e in (-2, 1, 0, -1)]
    goal += [(0, e) for e in (-2, 1, 0, -1)]
    goal += [(dy, e) for dy in ROWS for e in (-3, 2)] + [(0, -3), (0, 2)]
    goal = jnp.array(goal, i32)
    goal_req = ((y + goal[:, 0]) & (NY - 1)) * NZ + ((z + goal[:, 1]) & (NZ - 1))
    slot_of = jnp.sum(jnp.where(page_owner == me, page_slot, 0), axis=1)
    pick = goal_req[:, None] == jnp.arange(NY * NZ, dtype=i32)[None, :]
    slots = jnp.sum(jnp.where(pick, slot_of[None, :], 0), axis=1)

    rows = (0,) + ROWS
    use = [(role, -dy, 0) for role in (0, 1) for dy in rows]
    use += [(1, -dy, dz) for dz in (3, 1) for dy in rows]
    use += [(1, -dy, 2) for dy in rows]
    use += [(0, -dy, dz) for dz in (-3, -1) for dy in rows]
    use += [(0, -dy, -2) for dy in rows]
    table = jnp.array(use, i32)
    upper = table[:, 0] == 1
    owner = ((y + table[:, 1]) & (NY - 1)) * NZ + ((z + table[:, 2]) & (NZ - 1))
    below = y * NZ + ((z - 1) & (NZ - 1))

    def both(array):
        own = lax.dynamic_index_in_dim(array, me, 0, keepdims=True)
        other = lax.dynamic_index_in_dim(array, below, 0, keepdims=True)
        return jnp.where(upper.reshape((-1,) + (1,) * (own.ndim - 1)), other, own)

    number = jnp.arange(page_owner.shape[1], dtype=i32)[None, :]
    page_no = jnp.sum(jnp.where(both(page_owner) == owner[:, None], number, 0), axis=1)
    lims = jnp.clip(both(cached_len) - PAGE * page_no, 0, PAGE).astype(i32)

    m3, p3 = gather_pages(pool, slots, 0, (4, 4))
    far_m, far_p = shift(m3, 0, -3), shift(p3, 0, 3)
    *side_b, own_b = gather_pages(pool, slots, 8, (4, 4, 4, 4))
    b = [shift(x, dy, 0) for dy, x in zip(ROWS, side_b)]
    *side_a, own_a = gather_pages(pool, slots, 24, (2, 2, 2, 2))
    a = [shift(x, dy, 0) for dy, x in zip(ROWS, side_a)]

    m1, p1 = bundles([own_b] + b, ((0,), (1,)))
    m1, p1 = shift(m1, 0, -1), shift(p1, 0, 1)
    on = bundles([far_m, far_p], [((0, dy), (1, dy)) for dy in ROWS])
    f = [shift(x, dy, 0) for dy, x in zip(ROWS, on)]
    m2, p2 = bundles([own_a] + a, ((0,), (1,)))
    m2, p2 = shift(m2, 0, -2), shift(p2, 0, 2)

    four = [0, 1, 2, 3]
    low = [(own_b, [2])] + [(x, [2]) for x in b]
    upp = [(own_b, [3])] + [(x, [3]) for x in b]
    up = attend(q_up, None, lims, 4, upp, None, "state", unroll=2)
    home = attend(q, None, lims, 0, low, new_kv[0], "state", unroll=2)
    up = attend(
        q_up, up, lims, 8, [(far_m, [0])] + [(x, [0]) for x in f] + [(m1, four)], None, "state"
    )
    up = attend(q_up, up, lims, 16, [(m2, four)], None, "partial")
    back = shift(up, 0, -1)
    home = attend(
        q, home, lims, 20, [(far_p, [0])] + [(x, [1]) for x in f] + [(p1, four)], None, "state"
    )
    home = attend(q, home, lims, 28, [(p2, four)], None, "home", unroll=4)
    return merge(home, [back])[None]


def solution(mesh):
    split = P("pool", None, "head")
    return jax.shard_map(
        on_device,
        mesh=mesh,
        in_specs=(split, split, split, P(), P(), P()),
        out_specs=split,
        check_vma=False,
    )
```

profile of v0, /device:TPU:4, one launch (start us, length us, event | category | flops | bytes accessed | tf_op | source)
XLA Modules:
  0.0 154.6 jit_solution(5627180700642883224)
XLA Ops:
  1.8 2.2 %copy-done = bf16[32,256,256]{2,1,0:T(8,128)(2,1)S(1)} copy-done((bf16[32,256,256]{2,1,0:T(8,128)(2,1)S(1)}, bf16[32,256,256]{2,1,0:T(8,128)(2,1)}, u32[]{:S(2)}) %copy-start) | copy-done | bytes 4194328
  4.6 1.7 %collective-permute-start = (bf16[4,256,256]{2,1,0:T(8,128)(2,1)S(1)}, bf16[4,256,256]{2,1,0:T(8,128)(2,1)S(1)}, u32[]{:S(2)}, u32[]{:S(2)}) collective-permute-start(bf16[4,256,256]{2,1,0:T(8,128)(2,1)S(1)} %get-tuple-element.23), channel_id=1, source_target_pairs={{0,64},{8,72},{16,80},{24,88},{32,96},{40,104},{48,112},{56,120},{... | collective-permute-start | bytes 1572872 | tf_op jit(solution)/shard_map/ppermute | solution.py:210
  6.9 1.7 %collective-permute-start.9 = (bf16[2,256,256]{2,1,0:T(8,128)(2,1)S(1)}, bf16[2,256,256]{2,1,0:T(8,128)(2,1)S(1)}, u32[]{:S(2)}, u32[]{:S(2)}) collective-permute-start(bf16[2,256,256]{2,1,0:T(8,128)(2,1)S(1)} %get-tuple-element.33), channel_id=1, source_target_pairs={{0,64},{8,72},{16,80},{24,88},{32,96},{40,104},{48,112},{56,120},{... | collective-permute-start | bytes 786440 | tf_op jit(solution)/shard_map/ppermute | solution.py:210
  8.6 1.7 %collective-permute-start.10 = (bf16[2,256,256]{2,1,0:T(8,128)(2,1)S(1)}, bf16[2,256,256]{2,1,0:T(8,128)(2,1)S(1)}, u32[]{:S(2)}, u32[]{:S(2)}) collective-permute-start(bf16[2,256,256]{2,1,0:T(8,128)(2,1)S(1)} %get-tuple-element.34), channel_id=1, source_target_pairs={{0,192},{8,200},{16,208},{24,216},{32,224},{40,232},{48,240},{56,2... | collective-permute-start | bytes 786440 | tf_op jit(solution)/shard_map/ppermute | solution.py:210
  10.2 1.7 %collective-permute-start.11 = (bf16[2,256,256]{2,1,0:T(8,128)(2,1)S(1)}, bf16[2,256,256]{2,1,0:T(8,128)(2,1)S(1)}, u32[]{:S(2)}, u32[]{:S(2)}) collective-permute-start(bf16[2,256,256]{2,1,0:T(8,128)(2,1)S(1)} %get-tuple-element.35), channel_id=1, source_target_pairs={{0,128},{8,136},{16,144},{24,152},{32,160},{40,168},{48,176},{56,1... | collective-permute-start | bytes 786440 | tf_op jit(solution)/shard_map/ppermute | solution.py:210
  11.9 1.3 collective-permute-start.1
  13.3 12.0 %collective-permute-done.9.refs_1_ = bf16[2,256,256]{2,1,0:T(8,128)(2,1)S(1)} collective-permute-done((bf16[2,256,256]{2,1,0:T(8,128)(2,1)S(1)}, bf16[2,256,256]{2,1,0:T(8,128)(2,1)S(1)}, u32[]{:S(2)}, u32[]{:S(2)}) %collective-permute-start.9) | collective-permute-done | bytes 262176 | tf_op jit(solution)/shard_map/ppermute | solution.py:210
  25.3 13.2 %collective-permute-start.2 = (bf16[4,256,256]{2,1,0:T(8,128)(2,1)S(1)}, bf16[4,256,256]{2,1,0:T(8,128)(2,1)S(1)}, u32[]{:S(2)}, u32[]{:S(2)}) collective-permute-start(bf16[4,256,256]{2,1,0:T(8,128)(2,1)S(1)} %get-tuple-element.25), channel_id=1, source_target_pairs={{0,128},{8,136},{16,144},{24,152},{32,160},{40,168},{48,176},{56,1... | collective-permute-start | bytes 1572872 | tf_op jit(solution)/shard_map/ppermute | solution.py:210
  38.4 1.6 %shard_map.84 = (bf16[4,256,256]{2,1,0:T(8,128)(2,1)}, bf16[4,256,256]{2,1,0:T(8,128)(2,1)}) custom-call(s32[32]{0:T(128)S(1)} %select_reduce_fusion.slot_ref, bf16[32,256,256]{2,1,0:T(8,128)(2,1)S(1)} %copy-done), custom_call_target="tpu_custom_call" | custom-call | tf_op jit(solution)/shard_map/pallas_call | solution.py:26
  40.0 4.6 %collective-permute-start.3 = (bf16[4,256,256]{2,1,0:T(8,128)(2,1)}, bf16[4,256,256]{2,1,0:T(8,128)(2,1)}, u32[]{:S(2)}, u32[]{:S(2)}) collective-permute-start(bf16[4,256,256]{2,1,0:T(8,128)(2,1)} %get-tuple-element.26), channel_id=1, source_target_pairs={{0,24},{8,32},{16,40},{24,48},{32,56},{40,0},{48,8},{56,16},{64,88... | collective-permute-start | bytes 1572872 | tf_op jit(solution)/shard_map/ppermute | solution.py:210
  44.6 2.2 %collective-permute-start.4 = (bf16[4,256,256]{2,1,0:T(8,128)(2,1)}, bf16[4,256,256]{2,1,0:T(8,128)(2,1)}, u32[]{:S(2)}, u32[]{:S(2)}) collective-permute-start(bf16[4,256,256]{2,1,0:T(8,128)(2,1)} %get-tuple-element.27), channel_id=1, source_target_pairs={{0,40},{8,48},{16,56},{24,0},{32,8},{40,16},{48,24},{56,32},{64,10... | collective-permute-start | bytes 1572872 | tf_op jit(solution)/shard_map/ppermute | solution.py:210
  46.8 1.0 collective-permute-start.13
  51.2 2.2 %collective-permute-start.14 = (bf16[4,256,256]{2,1,0:T(8,128)(2,1)}, bf16[4,256,256]{2,1,0:T(8,128)(2,1)}, u32[]{:S(2)}, u32[]{:S(2)}) collective-permute-start(bf16[4,256,256]{2,1,0:T(8,128)(2,1)} %get-tuple-element.37), channel_id=1, source_target_pairs={{0,56},{8,0},{16,8},{24,16},{32,24},{40,32},{48,40},{56,48},{64,12... | collective-permute-start | bytes 1572872 | tf_op jit(solution)/shard_map/ppermute | solution.py:210
  53.4 3.3 %collective-permute-start.15 = (bf16[4,256,256]{2,1,0:T(8,128)(2,1)}, bf16[4,256,256]{2,1,0:T(8,128)(2,1)}, u32[]{:S(2)}, u32[]{:S(2)}) collective-permute-start(bf16[4,256,256]{2,1,0:T(8,128)(2,1)} %get-tuple-element.38), channel_id=1, source_target_pairs={{0,48},{8,56},{16,0},{24,8},{32,16},{40,24},{48,32},{56,40},{64,11... | collective-permute-start | bytes 1572872 | tf_op jit(solution)/shard_map/ppermute | solution.py:210
  57.5 14.2 %collective-permute-done.3.refs_1_ = bf16[4,256,256]{2,1,0:T(8,128)(2,1)} collective-permute-done((bf16[4,256,256]{2,1,0:T(8,128)(2,1)}, bf16[4,256,256]{2,1,0:T(8,128)(2,1)}, u32[]{:S(2)}, u32[]{:S(2)}) %collective-permute-start.3) | collective-permute-done | bytes 524320 | tf_op jit(solution)/shard_map/ppermute | solution.py:210
  71.7 3.8 %collective-permute-done.4.refs_0_.refs_1_ = bf16[4,256,256]{2,1,0:T(8,128)(2,1)} collective-permute-done((bf16[4,256,256]{2,1,0:T(8,128)(2,1)}, bf16[4,256,256]{2,1,0:T(8,128)(2,1)}, u32[]{:S(2)}, u32[]{:S(2)}) %collective-permute-start.4) | collective-permute-done | bytes 524320 | tf_op jit(solution)/shard_map/ppermute | solution.py:210
  75.5 1.3 shard_map.85
  76.8 3.2 %collective-permute-start.6 = (bf16[2,256,256]{2,1,0:T(8,128)(2,1)S(1)}, bf16[2,256,256]{2,1,0:T(8,128)(2,1)S(1)}, u32[]{:S(2)}, u32[]{:S(2)}) collective-permute-start(bf16[2,256,256]{2,1,0:T(8,128)(2,1)S(1)} %get-tuple-element.29), channel_id=1, source_target_pairs={{0,192},{8,200},{16,208},{24,216},{32,224},{40,232},{48,240},{56,2... | collective-permute-start | bytes 786440 | tf_op jit(solution)/shard_map/ppermute | solution.py:210
  80.1 1.0 collective-permute-start.7
  81.9 1.2 fusion.lim_ref
  83.1 5.2 %shard_map.91.refs_0_ = f32[8,256,256]{2,1,0:T(8,128)S(1)} custom-call(s32[32]{0:T(128)S(1)} %fusion.lim_ref, bf16[256,1024]{1,0:T(8,128)(2,1)S(1)} %collective-permute-done.13.q_ref, bf16[4,256,256]{2,1,0:T(8,128)(2,1)S(1)} %get-tuple-element.22.refs_1_.refs_0_, bf16[4,256,256]{2,1,0:T(8,128)(2,1)S(1)} %collective-permute-done.refs_2_.refs_1_, ...), custom_call_target="tpu_custom_call" | custom-call | tf_op jit(solution)/shard_map/pallas_call | solution.py:154
  89.2 8.6 %collective-permute-done.14.refs_5_ = bf16[4,256,256]{2,1,0:T(8,128)(2,1)} collective-permute-done((bf16[4,256,256]{2,1,0:T(8,128)(2,1)}, bf16[4,256,256]{2,1,0:T(8,128)(2,1)}, u32[]{:S(2)}, u32[]{:S(2)}) %collective-permute-start.14) | collective-permute-done | bytes 524320 | tf_op jit(solution)/shard_map/ppermute | solution.py:210
  97.8 8.1 %shard_map.92.refs_0_ = f32[8,256,256]{2,1,0:T(8,128)S(1)} custom-call(s32[32]{0:T(128)S(1)} %fusion.lim_ref, bf16[256,1024]{1,0:T(8,128)(2,1)S(1)} %collective-permute-done.13.q_ref, f32[8,256,256]{2,1,0:T(8,128)S(1)} %shard_map.91.refs_0_, bf16[4,256,256]{2,1,0:T(8,128)(2,1)} %collective-permute-done.4.refs_0_.refs_1_, ...), custom_call_target="tpu_custom_call", output_to_operand_aliasing={{}: (2, {})} | custom-call | tf_op jit(solution)/shard_map/pallas_call | solution.py:154
  106.0 5.0 %shard_map.93 = bf16[256,1152]{1,0:T(8,128)(2,1)S(1)} custom-call(s32[32]{0:T(128)S(1)} %fusion.lim_ref, bf16[256,1024]{1,0:T(8,128)(2,1)S(1)} %collective-permute-done.13.q_ref, f32[8,256,256]{2,1,0:T(8,128)S(1)} %shard_map.92.refs_0_, bf16[4,256,256]{2,1,0:T(8,128)(2,1)} %collective-permute-done.15.refs_1_), custom_call_target="tpu_custom_call" | custom-call | tf_op jit(solution)/shard_map/pallas_call | solution.py:154
  111.0 4.1 %collective-permute-start.16 = (bf16[256,1152]{1,0:T(8,128)(2,1)S(1)}, bf16[256,1152]{1,0:T(8,128)(2,1)S(1)}, u32[]{:S(2)}, u32[]{:S(2)}) collective-permute-start(bf16[256,1152]{1,0:T(8,128)(2,1)S(1)} %shard_map.93), channel_id=1, source_target_pairs={{0,56},{8,0},{16,8},{24,16},{32,24},{40,32},{48,40},{56,48},{64,12... | collective-permute-start | bytes 1769480 | tf_op jit(solution)/shard_map/ppermute | solution.py:210
  115.2 1.5 collective-permute-start.12
  116.7 6.2 %shard_map.83.refs_0_ = f32[8,256,256]{2,1,0:T(8,128)S(1)} custom-call(s32[32]{0:T(128)S(1)} %fusion.lim_ref, bf16[256,1024]{1,0:T(8,128)(2,1)S(1)} %bitcast.18, bf16[256,256]{1,0:T(8,128)(2,1)S(1)} %bitcast.21, bf16[4,256,256]{2,1,0:T(8,128)(2,1)S(1)} %get-tuple-element.22.refs_1_.refs_0_, bf16[4,256,256]{2,1,0:T(8,128)(2,1)S(1)} %collective-permute-done.refs_2_.refs_1_, ...), custom_call_target="tpu_custom_call" | custom-call | tf_op jit(solution)/shard_map/pallas_call | solution.py:154
  122.9 14.3 %collective-permute-done.8.refs_5_ = bf16[4,256,256]{2,1,0:T(8,128)(2,1)S(1)} collective-permute-done((bf16[4,256,256]{2,1,0:T(8,128)(2,1)S(1)}, bf16[4,256,256]{2,1,0:T(8,128)(2,1)S(1)}, u32[]{:S(2)}, u32[]{:S(2)}) %collective-permute-start.8) | collective-permute-done | bytes 524320 | tf_op jit(solution)/shard_map/ppermute | solution.py:210
  137.2 8.0 %shard_map.87.refs_0_ = f32[8,256,256]{2,1,0:T(8,128)S(1)} custom-call(s32[32]{0:T(128)S(1)} %fusion.lim_ref, bf16[256,1024]{1,0:T(8,128)(2,1)S(1)} %bitcast.19, f32[8,256,256]{2,1,0:T(8,128)S(1)} %shard_map.83.refs_0_, bf16[4,256,256]{2,1,0:T(8,128)(2,1)} %collective-permute-done.3.refs_1_, ...), custom_call_target="tpu_custom_call", output_to_operand_aliasing={{}: (2, {})} | custom-call | tf_op jit(solution)/shard_map/pallas_call | solution.py:154
  145.2 3.0 %collective-permute-done.12.refs_1_ = bf16[4,256,256]{2,1,0:T(8,128)(2,1)S(1)} collective-permute-done((bf16[4,256,256]{2,1,0:T(8,128)(2,1)S(1)}, bf16[4,256,256]{2,1,0:T(8,128)(2,1)S(1)}, u32[]{:S(2)}, u32[]{:S(2)}) %collective-permute-start.12) | collective-permute-done | bytes 524320 | tf_op jit(solution)/shard_map/ppermute | solution.py:210
  148.2 4.9 %shard_map.90.home_ref = f32[256,1152]{1,0:T(8,128)S(1)} custom-call(s32[32]{0:T(128)S(1)} %fusion.lim_ref, bf16[256,1024]{1,0:T(8,128)(2,1)S(1)} %bitcast.20, f32[8,256,256]{2,1,0:T(8,128)S(1)} %shard_map.87.refs_0_, bf16[4,256,256]{2,1,0:T(8,128)(2,1)S(1)} %collective-permute-done.12.refs_1_), custom_call_target="tpu_custom_call" | custom-call | tf_op jit(solution)/shard_map/pallas_call | solution.py:154
  153.0 1.6 %shard_map.94 = bf16[256,1024]{1,0:T(8,128)(2,1)} custom-call(f32[256,1152]{1,0:T(8,128)S(1)} %shard_map.90.home_ref, bf16[256,1152]{1,0:T(8,128)(2,1)S(1)} %collective-permute-done.16.refs_0_), custom_call_target="tpu_custom_call" | custom-call | tf_op jit(solution)/shard_map/pallas_call | solution.py:197
  (42 shorter events, 8.9 us)
Async XLA Ops:
  1.7 2.2 %copy-start = (bf16[32,256,256]{2,1,0:T(8,128)(2,1)S(1)}, bf16[32,256,256]{2,1,0:T(8,128)(2,1)}, u32[]{:S(2)}) copy-start(bf16[32,256,256]{2,1,0:T(8,128)(2,1)} %pool_ref.5) | copy-start | bytes 12582916
  4.6 42.2 %collective-permute-start = (bf16[4,256,256]{2,1,0:T(8,128)(2,1)S(1)}, bf16[4,256,256]{2,1,0:T(8,128)(2,1)S(1)}, u32[]{:S(2)}, u32[]{:S(2)}) collective-permute-start(bf16[4,256,256]{2,1,0:T(8,128)(2,1)S(1)} %get-tuple-element.23), channel_id=1, source_target_pairs={{0,64},{8,72},{16,80},{24,88},{32,96},{40,104},{48,112},{56,120},{... | collective-permute-start | bytes 1572872 | tf_op jit(solution)/shard_map/ppermute | solution.py:210
  6.9 18.4 %collective-permute-start.9 = (bf16[2,256,256]{2,1,0:T(8,128)(2,1)S(1)}, bf16[2,256,256]{2,1,0:T(8,128)(2,1)S(1)}, u32[]{:S(2)}, u32[]{:S(2)}) collective-permute-start(bf16[2,256,256]{2,1,0:T(8,128)(2,1)S(1)} %get-tuple-element.33), channel_id=1, source_target_pairs={{0,64},{8,72},{16,80},{24,88},{32,96},{40,104},{48,112},{56,120},{... | collective-permute-start | bytes 786440 | tf_op jit(solution)/shard_map/ppermute | solution.py:210
  8.6 31.4 %collective-permute-start.10 = (bf16[2,256,256]{2,1,0:T(8,128)(2,1)S(1)}, bf16[2,256,256]{2,1,0:T(8,128)(2,1)S(1)}, u32[]{:S(2)}, u32[]{:S(2)}) collective-permute-start(bf16[2,256,256]{2,1,0:T(8,128)(2,1)S(1)} %get-tuple-element.34), channel_id=1, source_target_pairs={{0,192},{8,200},{16,208},{24,216},{32,224},{40,232},{48,240},{56,2... | collective-permute-start | bytes 786440 | tf_op jit(solution)/shard_map/ppermute | solution.py:210
  10.2 34.4 %collective-permute-start.11 = (bf16[2,256,256]{2,1,0:T(8,128)(2,1)S(1)}, bf16[2,256,256]{2,1,0:T(8,128)(2,1)S(1)}, u32[]{:S(2)}, u32[]{:S(2)}) collective-permute-start(bf16[2,256,256]{2,1,0:T(8,128)(2,1)S(1)} %get-tuple-element.35), channel_id=1, source_target_pairs={{0,128},{8,136},{16,144},{24,152},{32,160},{40,168},{48,176},{56,1... | collective-permute-start | bytes 786440 | tf_op jit(solution)/shard_map/ppermute | solution.py:210
  11.9 37.6 %collective-permute-start.1 = (bf16[4,256,256]{2,1,0:T(8,128)(2,1)S(1)}, bf16[4,256,256]{2,1,0:T(8,128)(2,1)S(1)}, u32[]{:S(2)}, u32[]{:S(2)}) collective-permute-start(bf16[4,256,256]{2,1,0:T(8,128)(2,1)S(1)} %get-tuple-element.24), channel_id=1, source_target_pairs={{0,192},{8,200},{16,208},{24,216},{32,224},{40,232},{48,240},{56,2... | collective-permute-start | bytes 1572872 | tf_op jit(solution)/shard_map/ppermute | solution.py:210
  25.3 21.6 %copy-start.1 = (bf16[1,256,1024]{2,1,0:T(8,128)(2,1)S(1)}, bf16[1,256,1024]{2,1,0:T(8,128)(2,1)}, u32[]{:S(2)}) copy-start(bf16[1,256,1024]{2,1,0:T(8,128)(2,1)} %param.8) | copy-start | bytes 1572868
  25.3 24.3 %collective-permute-start.2 = (bf16[4,256,256]{2,1,0:T(8,128)(2,1)S(1)}, bf16[4,256,256]{2,1,0:T(8,128)(2,1)S(1)}, u32[]{:S(2)}, u32[]{:S(2)}) collective-permute-start(bf16[4,256,256]{2,1,0:T(8,128)(2,1)S(1)} %get-tuple-element.25), channel_id=1, source_target_pairs={{0,128},{8,136},{16,144},{24,152},{32,160},{40,168},{48,176},{56,1... | collective-permute-start | bytes 1572872 | tf_op jit(solution)/shard_map/ppermute | solution.py:210
  40.0 31.7 %collective-permute-start.3 = (bf16[4,256,256]{2,1,0:T(8,128)(2,1)}, bf16[4,256,256]{2,1,0:T(8,128)(2,1)}, u32[]{:S(2)}, u32[]{:S(2)}) collective-permute-start(bf16[4,256,256]{2,1,0:T(8,128)(2,1)} %get-tuple-element.26), channel_id=1, source_target_pairs={{0,24},{8,32},{16,40},{24,48},{32,56},{40,0},{48,8},{56,16},{64,88... | collective-permute-start | bytes 1572872 | tf_op jit(solution)/shard_map/ppermute | solution.py:210
  44.6 30.9 %collective-permute-start.4 = (bf16[4,256,256]{2,1,0:T(8,128)(2,1)}, bf16[4,256,256]{2,1,0:T(8,128)(2,1)}, u32[]{:S(2)}, u32[]{:S(2)}) collective-permute-start(bf16[4,256,256]{2,1,0:T(8,128)(2,1)} %get-tuple-element.27), channel_id=1, source_target_pairs={{0,40},{8,48},{16,56},{24,0},{32,8},{40,16},{48,24},{56,32},{64,10... | collective-permute-start | bytes 1572872 | tf_op jit(solution)/shard_map/ppermute | solution.py:210
  46.8 33.2 %collective-permute-start.13 = (bf16[256,1024]{1,0:T(8,128)(2,1)S(1)}, bf16[256,1024]{1,0:T(8,128)(2,1)S(1)}, u32[]{:S(2)}, u32[]{:S(2)}) collective-permute-start(bf16[256,1024]{1,0:T(8,128)(2,1)S(1)} %bitcast.17), channel_id=1, source_target_pairs={{0,8},{8,16},{16,24},{24,32},{32,40},{40,48},{48,56},{56,0},{64,72... | collective-permute-start | bytes 1572872 | tf_op jit(solution)/shard_map/ppermute | solution.py:210
  47.9 33.3 %copy-start.9 = (pred[32]{0:T(512)(128)(4,1)S(1)}, pred[32]{0:T(512)(128)(4,1)}, u32[]{:S(2)}) copy-start(pred[32]{0:T(512)(128)(4,1)} %constant.48) | copy-start | bytes 100
  47.9 33.4 %copy-start.7 = (s32[32]{0:T(128)S(1)}, s32[32]{0:T(128)}, u32[]{:S(2)}) copy-start(s32[32]{0:T(128)} %param.13) | copy-start | bytes 388
  47.9 34.0 %copy-start.8 = (pred[32,1]{0,1:T(4,128)(4,1)S(1)}, pred[32,1]{0,1:T(4,128)(4,1)}, u32[]{:S(2)}) copy-start(pred[32,1]{0,1:T(4,128)(4,1)} %constant.47) | copy-start | bytes 100
  48.7 0.8 copy-start.3
  50.4 0.8 copy-start.5
  51.2 46.6 %collective-permute-start.14 = (bf16[4,256,256]{2,1,0:T(8,128)(2,1)}, bf16[4,256,256]{2,1,0:T(8,128)(2,1)}, u32[]{:S(2)}, u32[]{:S(2)}) collective-permute-start(bf16[4,256,256]{2,1,0:T(8,128)(2,1)} %get-tuple-element.37), channel_id=1, source_target_pairs={{0,56},{8,0},{16,8},{24,16},{32,24},{40,32},{48,40},{56,48},{64,12... | collective-permute-start | bytes 1572872 | tf_op jit(solution)/shard_map/ppermute | solution.py:210
  53.4 52.6 %collective-permute-start.15 = (bf16[4,256,256]{2,1,0:T(8,128)(2,1)}, bf16[4,256,256]{2,1,0:T(8,128)(2,1)}, u32[]{:S(2)}, u32[]{:S(2)}) collective-permute-start(bf16[4,256,256]{2,1,0:T(8,128)(2,1)} %get-tuple-element.38), channel_id=1, source_target_pairs={{0,48},{8,56},{16,0},{24,8},{32,16},{40,24},{48,32},{56,40},{64,11... | collective-permute-start | bytes 1572872 | tf_op jit(solution)/shard_map/ppermute | solution.py:210
  76.7 12.0 %collective-permute-start.5 = (bf16[2,256,256]{2,1,0:T(8,128)(2,1)S(1)}, bf16[2,256,256]{2,1,0:T(8,128)(2,1)S(1)}, u32[]{:S(2)}, u32[]{:S(2)}) collective-permute-start(bf16[2,256,256]{2,1,0:T(8,128)(2,1)S(1)} %get-tuple-element.28), channel_id=1, source_target_pairs={{0,64},{8,72},{16,80},{24,88},{32,96},{40,104},{48,112},{56,120},{... | collective-permute-start | bytes 786440 | tf_op jit(solution)/shard_map/ppermute | solution.py:210
  76.8 12.4 %collective-permute-start.6 = (bf16[2,256,256]{2,1,0:T(8,128)(2,1)S(1)}, bf16[2,256,256]{2,1,0:T(8,128)(2,1)S(1)}, u32[]{:S(2)}, u32[]{:S(2)}) collective-permute-start(bf16[2,256,256]{2,1,0:T(8,128)(2,1)S(1)} %get-tuple-element.29), channel_id=1, source_target_pairs={{0,192},{8,200},{16,208},{24,216},{32,224},{40,232},{48,240},{56,2... | collective-permute-start | bytes 786440 | tf_op jit(solution)/shard_map/ppermute | solution.py:210
  80.1 9.2 %collective-permute-start.7 = (bf16[2,256,256]{2,1,0:T(8,128)(2,1)S(1)}, bf16[2,256,256]{2,1,0:T(8,128)(2,1)S(1)}, u32[]{:S(2)}, u32[]{:S(2)}) collective-permute-start(bf16[2,256,256]{2,1,0:T(8,128)(2,1)S(1)} %get-tuple-element.30), channel_id=1, source_target_pairs={{0,128},{8,136},{16,144},{24,152},{32,160},{40,168},{48,176},{56,1... | collective-permute-start | bytes 786440 | tf_op jit(solution)/shard_map/ppermute | solution.py:210
  106.0 9.2 %copy-start.6 = (bf16[4,256,256]{2,1,0:T(8,128)(2,1)S(1)}, bf16[4,256,256]{2,1,0:T(8,128)(2,1)}, u32[]{:S(2)}) copy-start(bf16[4,256,256]{2,1,0:T(8,128)(2,1)} %copy-done.5) | copy-start | bytes 1572868
  106.0 9.2 %copy-start.4 = (bf16[4,256,256]{2,1,0:T(8,128)(2,1)S(1)}, bf16[4,256,256]{2,1,0:T(8,128)(2,1)}, u32[]{:S(2)}) copy-start(bf16[4,256,256]{2,1,0:T(8,128)(2,1)} %copy-done.3) | copy-start | bytes 1572868
  106.0 10.7 %copy-start.2 = (bf16[1,256,256]{2,1,0:T(8,128)(2,1)S(1)}, bf16[1,256,256]{2,1,0:T(8,128)(2,1)}, u32[]{:S(2)}) copy-start(bf16[1,256,256]{2,1,0:T(8,128)(2,1)} %param.9) | copy-start | bytes 393220
  111.0 42.0 %collective-permute-start.16 = (bf16[256,1152]{1,0:T(8,128)(2,1)S(1)}, bf16[256,1152]{1,0:T(8,128)(2,1)S(1)}, u32[]{:S(2)}, u32[]{:S(2)}) collective-permute-start(bf16[256,1152]{1,0:T(8,128)(2,1)S(1)} %shard_map.93), channel_id=1, source_target_pairs={{0,56},{8,0},{16,8},{24,16},{32,24},{40,32},{48,40},{56,48},{64,12... | collective-permute-start | bytes 1769480 | tf_op jit(solution)/shard_map/ppermute | solution.py:210
  115.2 22.0 %collective-permute-start.8 = (bf16[4,256,256]{2,1,0:T(8,128)(2,1)S(1)}, bf16[4,256,256]{2,1,0:T(8,128)(2,1)S(1)}, u32[]{:S(2)}, u32[]{:S(2)}) collective-permute-start(bf16[4,256,256]{2,1,0:T(8,128)(2,1)S(1)} %copy-done.6), channel_id=1, source_target_pairs={{0,8},{8,16},{16,24},{24,32},{32,40},{40,48},{48,56},{56,0},{64,72... | collective-permute-start | bytes 1572872 | tf_op jit(solution)/shard_map/ppermute | solution.py:210
  115.2 33.0 %collective-permute-start.12 = (bf16[4,256,256]{2,1,0:T(8,128)(2,1)S(1)}, bf16[4,256,256]{2,1,0:T(8,128)(2,1)S(1)}, u32[]{:S(2)}, u32[]{:S(2)}) collective-permute-start(bf16[4,256,256]{2,1,0:T(8,128)(2,1)S(1)} %copy-done.4), channel_id=1, source_target_pairs={{0,16},{8,24},{16,32},{24,40},{32,48},{40,56},{48,0},{56,8},{64,80... | collective-permute-start | bytes 1572872 | tf_op jit(solution)/shard_map/ppermute | solution.py:210
where the time goes:
time: 155 us
  waiting for transfers between devices  56.8 us (37%)
  Pallas kernels  44.8 us (29%)
  starting transfers between devices  44.5 us (29%)
  local copies, waits for them, and re-layouts  5.19 us (3%)
  other arithmetic  3.14 us (2%)
    ppermute x17, waiting for transfers between devices, shift(): return lax.ppermute(x, 'pool', pairs)  56.8 us
    ppermute x17, starting transfers between devices, shift(): return lax.ppermute(x, 'pool', pairs)  44.5 us
    pallas_call x6, Pallas kernels, attend(): pl.pallas_call(body, in_specs=[pl.BlockSpec(memory_space=pltpu.SMEM)] + [...  37.4 us
    unnamed x20, local copies, waits for them, and re-layouts  3.82 us
  transfers between devices with their start and end apart: 17, of which 8 were waited for; matrix products, arithmetic and copies ran while one was open for 2% of the time, Pallas kernels for 24%

commit v1 on v0

--- a/solution.py
+++ b/solution.py
@@ -234,9 +234,9 @@
 
     rows = (0,) + ROWS
     use = [(role, -dy, 0) for role in (0, 1) for dy in rows]
-    use += [(1, -dy, dz) for dz in (3, 1) for dy in rows]
+    use += [(1, -dy, dz) for dz in (1, 3) for dy in rows]
     use += [(1, -dy, 2) for dy in rows]
-    use += [(0, -dy, dz) for dz in (-3, -1) for dy in rows]
+    use += [(0, -dy, dz) for dz in (-1, -3) for dy in rows]
     use += [(0, -dy, -2) for dy in rows]
     table = jnp.array(use, i32)
     upper = table[:, 0] == 1
@@ -269,15 +269,15 @@
     four = [0, 1, 2, 3]
     low = [(own_b, [2])] + [(x, [2]) for x in b]
     upp = [(own_b, [3])] + [(x, [3]) for x in b]
-    up = attend(q_up, None, lims, 4, upp, None, "state", unroll=2)
+    upp.append((m1, four))
     home = attend(q, None, lims, 0, low, new_kv[0], "state", unroll=2)
-    up = attend(
-        q_up, up, lims, 8, [(far_m, [0])] + [(x, [0]) for x in f] + [(m1, four)], None, "state"
-    )
+    up = attend(q_up, None, lims, 4, upp, None, "state")
+    home = attend(q, home, lims, 20, [(p1, four)], None, "state", unroll=4)
+    up = attend(q_up, up, lims, 12, [(far_m, [0])] + [(x, [0]) for x in f], None, "state")
     up = attend(q_up, up, lims, 16, [(m2, four)], None, "partial")
     back = shift(up, 0, -1)
     home = attend(
-        q, home, lims, 20, [(far_p, [0])] + [(x, [1]) for x in f] + [(p1, four)], None, "state"
+        q, home, lims, 24, [(far_p, [0])] + [(x, [1]) for x in f], None, "state", unroll=4
     )
     home = attend(q, home, lims, 28, [(p2, four)], None, "home", unroll=4)
     return merge(home, [back])[None]

time: 155 us -> 163 us (1.052)
  waiting for transfers between devices: 56.8 us -> 75.1 us
  starting transfers between devices: 44.5 us -> 31 us
  Pallas kernels: 44.8 us -> 48.2 us
    ppermute x17, waiting for transfers between devices: 56.8 us -> 75.1 us  [shift(): return lax.ppermute(x, 'pool', pairs)]
    ppermute x17, starting transfers between devices: 44.5 us -> 31 us  [shift(): return lax.ppermute(x, 'pool', pairs)]
    pallas_call x6 -> x7, Pallas kernels: 37.4 us -> 40.8 us  [attend(): pl.pallas_call(body, in_specs=[pl.BlockSpec(memory_space=pltpu.SMEM)] + [...]
  transfers between devices with their start and end apart: 17 -> 17, of which waited for: 8 -> 6; matrix products, arithmetic and copies ran while one was open for 2% -> 2% of each run, Pallas kernels for 24% -> 25%
where the time goes in v1:
time: 163 us; the launch traced here: 162 us
  waiting for transfers between devices  75.1 us (46%)
  Pallas kernels  48.2 us (30%)
  starting transfers between devices  31 us (19%)
  local copies, waits for them, and re-layouts  4.45 us (3%)
  other arithmetic  3.24 us (2%)
    ppermute x17, waiting for transfers between devices, shift(): return lax.ppermute(x, 'pool', pairs)  75.1 us
    pallas_call x7, Pallas kernels, attend(): pl.pallas_call(body, in_specs=[pl.BlockSpec(memory_space=pltpu.SMEM)] + [...  40.8 us
    ppermute x17, starting transfers between devices, shift(): return lax.ppermute(x, 'pool', pairs)  31 us
  transfers between devices with their start and end apart: 17, of which 6 were waited for; matrix products, arithmetic and copies ran while one was open for 2% of the time, Pallas kernels for 25%

profile of v1, /device:TPU:4, one launch (start us, length us, event | category | flops | bytes accessed | tf_op | source)
XLA Modules:
  0.0 162.2 jit_solution(4071719834104581898)
XLA Ops:
  0.0 0.8 select_reduce_fusion.1
  1.8 2.2 %copy-done = bf16[32,256,256]{2,1,0:T(8,128)(2,1)S(1)} copy-done((bf16[32,256,256]{2,1,0:T(8,128)(2,1)S(1)}, bf16[32,256,256]{2,1,0:T(8,128)(2,1)}, u32[]{:S(2)}) %copy-start) | copy-done | bytes 4194328
  4.6 1.7 %collective-permute-start = (bf16[4,256,256]{2,1,0:T(8,128)(2,1)S(1)}, bf16[4,256,256]{2,1,0:T(8,128)(2,1)S(1)}, u32[]{:S(2)}, u32[]{:S(2)}) collective-permute-start(bf16[4,256,256]{2,1,0:T(8,128)(2,1)S(1)} %get-tuple-element.23), channel_id=1, source_target_pairs={{0,64},{8,72},{16,80},{24,88},{32,96},{40,104},{48,112},{56,120},{... | collective-permute-start | bytes 1572872 | tf_op jit(solution)/shard_map/ppermute | solution.py:210
  6.3 1.7 %collective-permute-start.1 = (bf16[4,256,256]{2,1,0:T(8,128)(2,1)S(1)}, bf16[4,256,256]{2,1,0:T(8,128)(2,1)S(1)}, u32[]{:S(2)}, u32[]{:S(2)}) collective-permute-start(bf16[4,256,256]{2,1,0:T(8,128)(2,1)S(1)} %get-tuple-element.24), channel_id=1, source_target_pairs={{0,192},{8,200},{16,208},{24,216},{32,224},{40,232},{48,240},{56,2... | collective-permute-start | bytes 1572872 | tf_op jit(solution)/shard_map/ppermute | solution.py:210
  7.9 2.0 %collective-permute-start.2 = (bf16[4,256,256]{2,1,0:T(8,128)(2,1)S(1)}, bf16[4,256,256]{2,1,0:T(8,128)(2,1)S(1)}, u32[]{:S(2)}, u32[]{:S(2)}) collective-permute-start(bf16[4,256,256]{2,1,0:T(8,128)(2,1)S(1)} %get-tuple-element.25), channel_id=1, source_target_pairs={{0,128},{8,136},{16,144},{24,152},{32,160},{40,168},{48,176},{56,1... | collective-permute-start | bytes 1572872 | tf_op jit(solution)/shard_map/ppermute | solution.py:210
  11.3 1.6 shard_map.86
  12.9 4.6 %collective-permute-start.4 = (bf16[4,256,256]{2,1,0:T(8,128)(2,1)}, bf16[4,256,256]{2,1,0:T(8,128)(2,1)}, u32[]{:S(2)}, u32[]{:S(2)}) collective-permute-start(bf16[4,256,256]{2,1,0:T(8,128)(2,1)} %get-tuple-element.27), channel_id=1, source_target_pairs={{0,24},{8,32},{16,40},{24,48},{32,56},{40,0},{48,8},{56,16},{64,88... | collective-permute-start | bytes 1572872 | tf_op jit(solution)/shard_map/ppermute | solution.py:210
  17.5 19.0 %collective-permute-done.9.refs_1_ = bf16[2,256,256]{2,1,0:T(8,128)(2,1)S(1)} collective-permute-done((bf16[2,256,256]{2,1,0:T(8,128)(2,1)S(1)}, bf16[2,256,256]{2,1,0:T(8,128)(2,1)S(1)}, u32[]{:S(2)}, u32[]{:S(2)}) %collective-permute-start.9) | collective-permute-done | bytes 262176 | tf_op jit(solution)/shard_map/ppermute | solution.py:210
  36.5 6.7 %collective-permute-start.5 = (bf16[4,256,256]{2,1,0:T(8,128)(2,1)}, bf16[4,256,256]{2,1,0:T(8,128)(2,1)}, u32[]{:S(2)}, u32[]{:S(2)}) collective-permute-start(bf16[4,256,256]{2,1,0:T(8,128)(2,1)} %get-tuple-element.28), channel_id=1, source_target_pairs={{0,40},{8,48},{16,56},{24,0},{32,8},{40,16},{48,24},{56,32},{64,10... | collective-permute-start | bytes 1572872 | tf_op jit(solution)/shard_map/ppermute | solution.py:210
  43.2 1.0 collective-permute-start.13
  44.3 1.8 %collective-permute-start.10 = (bf16[2,256,256]{2,1,0:T(8,128)(2,1)S(1)}, bf16[2,256,256]{2,1,0:T(8,128)(2,1)S(1)}, u32[]{:S(2)}, u32[]{:S(2)}) collective-permute-start(bf16[2,256,256]{2,1,0:T(8,128)(2,1)S(1)} %get-tuple-element.34), channel_id=1, source_target_pairs={{0,192},{8,200},{16,208},{24,216},{32,224},{40,232},{48,240},{56,2... | collective-permute-start | bytes 786440 | tf_op jit(solution)/shard_map/ppermute | solution.py:210
  46.7 0.9 shard_map.84
  47.6 5.9 %collective-permute-done.10.refs_2_ = bf16[2,256,256]{2,1,0:T(8,128)(2,1)S(1)} collective-permute-done((bf16[2,256,256]{2,1,0:T(8,128)(2,1)S(1)}, bf16[2,256,256]{2,1,0:T(8,128)(2,1)S(1)}, u32[]{:S(2)}, u32[]{:S(2)}) %collective-permute-start.10) | collective-permute-done | bytes 262176 | tf_op jit(solution)/shard_map/ppermute | solution.py:210
  53.4 2.2 %collective-permute-start.14 = (bf16[4,256,256]{2,1,0:T(8,128)(2,1)}, bf16[4,256,256]{2,1,0:T(8,128)(2,1)}, u32[]{:S(2)}, u32[]{:S(2)}) collective-permute-start(bf16[4,256,256]{2,1,0:T(8,128)(2,1)} %get-tuple-element.37), channel_id=1, source_target_pairs={{0,56},{8,0},{16,8},{24,16},{32,24},{40,32},{48,40},{56,48},{64,12... | collective-permute-start | bytes 1572872 | tf_op jit(solution)/shard_map/ppermute | solution.py:210
  55.7 0.9 shard_map.90
  56.5 0.8 copy-done.5
  58.1 19.1 %collective-permute-done.5.refs_0_.refs_1_ = bf16[4,256,256]{2,1,0:T(8,128)(2,1)} collective-permute-done((bf16[4,256,256]{2,1,0:T(8,128)(2,1)}, bf16[4,256,256]{2,1,0:T(8,128)(2,1)}, u32[]{:S(2)}, u32[]{:S(2)}) %collective-permute-start.5) | collective-permute-done | bytes 524320 | tf_op jit(solution)/shard_map/ppermute | solution.py:210
  77.2 1.3 shard_map.87
  78.8 2.9 %collective-permute-start.7 = (bf16[2,256,256]{2,1,0:T(8,128)(2,1)S(1)}, bf16[2,256,256]{2,1,0:T(8,128)(2,1)S(1)}, u32[]{:S(2)}, u32[]{:S(2)}) collective-permute-start(bf16[2,256,256]{2,1,0:T(8,128)(2,1)S(1)} %get-tuple-element.30), channel_id=1, source_target_pairs={{0,192},{8,200},{16,208},{24,216},{32,224},{40,232},{48,240},{56,2... | collective-permute-start | bytes 786440 | tf_op jit(solution)/shard_map/ppermute | solution.py:210
  83.3 1.3 fusion.lim_ref
  84.6 14.9 %collective-permute-done.14.refs_4_ = bf16[4,256,256]{2,1,0:T(8,128)(2,1)} collective-permute-done((bf16[4,256,256]{2,1,0:T(8,128)(2,1)}, bf16[4,256,256]{2,1,0:T(8,128)(2,1)}, u32[]{:S(2)}, u32[]{:S(2)}) %collective-permute-start.14) | collective-permute-done | bytes 524320 | tf_op jit(solution)/shard_map/ppermute | solution.py:210
  99.6 7.0 %shard_map.92.refs_0_ = f32[8,256,256]{2,1,0:T(8,128)S(1)} custom-call(s32[32]{0:T(128)S(1)} %fusion.lim_ref, bf16[256,1024]{1,0:T(8,128)(2,1)S(1)} %collective-permute-done.13.q_ref, bf16[4,256,256]{2,1,0:T(8,128)(2,1)S(1)} %get-tuple-element.22.refs_1_.refs_0_, bf16[4,256,256]{2,1,0:T(8,128)(2,1)S(1)} %collective-permute-done.refs_2_.refs_1_, ...), custom_call_target="tpu_custom_call" | custom-call | tf_op jit(solution)/shard_map/pallas_call | solution.py:154
  106.6 5.1 %shard_map.93.refs_0_ = f32[8,256,256]{2,1,0:T(8,128)S(1)} custom-call(s32[32]{0:T(128)S(1)} %fusion.lim_ref, bf16[256,1024]{1,0:T(8,128)(2,1)S(1)} %collective-permute-done.13.q_ref, f32[8,256,256]{2,1,0:T(8,128)S(1)} %shard_map.92.refs_0_, bf16[4,256,256]{2,1,0:T(8,128)(2,1)} %collective-permute-done.5.refs_0_.refs_1_, ...), custom_call_target="tpu_custom_call", output_to_operand_aliasing={{}: (2, {})} | custom-call | tf_op jit(solution)/shard_map/pallas_call | solution.py:154
  111.7 5.3 %shard_map.94 = bf16[256,1152]{1,0:T(8,128)(2,1)S(1)} custom-call(s32[32]{0:T(128)S(1)} %fusion.lim_ref, bf16[256,1024]{1,0:T(8,128)(2,1)S(1)} %collective-permute-done.13.q_ref, f32[8,256,256]{2,1,0:T(8,128)S(1)} %shard_map.93.refs_0_, bf16[4,256,256]{2,1,0:T(8,128)(2,1)} %collective-permute-done.15.refs_1_), custom_call_target="tpu_custom_call" | custom-call | tf_op jit(solution)/shard_map/pallas_call | solution.py:154
  117.0 3.9 %collective-permute-start.16 = (bf16[256,1152]{1,0:T(8,128)(2,1)S(1)}, bf16[256,1152]{1,0:T(8,128)(2,1)S(1)}, u32[]{:S(2)}, u32[]{:S(2)}) collective-permute-start(bf16[256,1152]{1,0:T(8,128)(2,1)S(1)} %shard_map.94), channel_id=1, source_target_pairs={{0,56},{8,0},{16,8},{24,16},{32,24},{40,32},{48,40},{56,48},{64,12... | collective-permute-start | bytes 1769480 | tf_op jit(solution)/shard_map/ppermute | solution.py:210
  121.0 6.2 %shard_map.83.refs_0_ = f32[8,256,256]{2,1,0:T(8,128)S(1)} custom-call(s32[32]{0:T(128)S(1)} %fusion.lim_ref, bf16[256,1024]{1,0:T(8,128)(2,1)S(1)} %bitcast.18, bf16[256,256]{1,0:T(8,128)(2,1)S(1)} %bitcast.22, bf16[4,256,256]{2,1,0:T(8,128)(2,1)S(1)} %get-tuple-element.22.refs_1_.refs_0_, bf16[4,256,256]{2,1,0:T(8,128)(2,1)S(1)} %collective-permute-done.refs_2_.refs_1_, ...), custom_call_target="tpu_custom_call" | custom-call | tf_op jit(solution)/shard_map/pallas_call | solution.py:154
  127.2 15.1 %collective-permute-done.3.refs_1_ = bf16[4,256,256]{2,1,0:T(8,128)(2,1)S(1)} collective-permute-done((bf16[4,256,256]{2,1,0:T(8,128)(2,1)S(1)}, bf16[4,256,256]{2,1,0:T(8,128)(2,1)S(1)}, u32[]{:S(2)}, u32[]{:S(2)}) %collective-permute-start.3) | collective-permute-done | bytes 524320 | tf_op jit(solution)/shard_map/ppermute | solution.py:210
  142.3 6.0 %shard_map.85.refs_0_ = f32[8,256,256]{2,1,0:T(8,128)S(1)} custom-call(s32[32]{0:T(128)S(1)} %fusion.lim_ref, bf16[256,1024]{1,0:T(8,128)(2,1)S(1)} %bitcast.19, f32[8,256,256]{2,1,0:T(8,128)S(1)} %shard_map.83.refs_0_, bf16[4,256,256]{2,1,0:T(8,128)(2,1)S(1)} %collective-permute-done.3.refs_1_), custom_call_target="tpu_custom_call", output_to_operand_aliasing={{}: (2, {})} | custom-call | tf_op jit(solution)/shard_map/pallas_call | solution.py:154
  148.3 6.5 %shard_map.88.refs_0_ = f32[8,256,256]{2,1,0:T(8,128)S(1)} custom-call(s32[32]{0:T(128)S(1)} %fusion.lim_ref, bf16[256,1024]{1,0:T(8,128)(2,1)S(1)} %bitcast.20, f32[8,256,256]{2,1,0:T(8,128)S(1)} %shard_map.85.refs_0_, bf16[4,256,256]{2,1,0:T(8,128)(2,1)} %collective-permute-done.4.refs_1_, ...), custom_call_target="tpu_custom_call", output_to_operand_aliasing={{}: (2, {})} | custom-call | tf_op jit(solution)/shard_map/pallas_call | solution.py:154
  154.7 1.1 collective-permute-done.12.refs_1_
  155.8 4.9 %shard_map.91.home_ref = f32[256,1152]{1,0:T(8,128)S(1)} custom-call(s32[32]{0:T(128)S(1)} %fusion.lim_ref, bf16[256,1024]{1,0:T(8,128)(2,1)S(1)} %bitcast.21, f32[8,256,256]{2,1,0:T(8,128)S(1)} %shard_map.88.refs_0_, bf16[4,256,256]{2,1,0:T(8,128)(2,1)S(1)} %collective-permute-done.12.refs_1_), custom_call_target="tpu_custom_call" | custom-call | tf_op jit(solution)/shard_map/pallas_call | solution.py:154
  160.7 1.6 shard_map.95
  (43 shorter events, 6.4 us)
Async XLA Ops:
  1.7 2.2 %copy-start = (bf16[32,256,256]{2,1,0:T(8,128)(2,1)S(1)}, bf16[32,256,256]{2,1,0:T(8,128)(2,1)}, u32[]{:S(2)}) copy-start(bf16[32,256,256]{2,1,0:T(8,128)(2,1)} %pool_ref.5) | copy-start | bytes 12582916
  4.6 38.6 %collective-permute-start = (bf16[4,256,256]{2,1,0:T(8,128)(2,1)S(1)}, bf16[4,256,256]{2,1,0:T(8,128)(2,1)S(1)}, u32[]{:S(2)}, u32[]{:S(2)}) collective-permute-start(bf16[4,256,256]{2,1,0:T(8,128)(2,1)S(1)} %get-tuple-element.23), channel_id=1, source_target_pairs={{0,64},{8,72},{16,80},{24,88},{32,96},{40,104},{48,112},{56,120},{... | collective-permute-start | bytes 1572872 | tf_op jit(solution)/shard_map/ppermute | solution.py:210
  6.3 38.0 %collective-permute-start.1 = (bf16[4,256,256]{2,1,0:T(8,128)(2,1)S(1)}, bf16[4,256,256]{2,1,0:T(8,128)(2,1)S(1)}, u32[]{:S(2)}, u32[]{:S(2)}) collective-permute-start(bf16[4,256,256]{2,1,0:T(8,128)(2,1)S(1)} %get-tuple-element.24), channel_id=1, source_target_pairs={{0,192},{8,200},{16,208},{24,216},{32,224},{40,232},{48,240},{56,2... | collective-permute-start | bytes 1572872 | tf_op jit(solution)/shard_map/ppermute | solution.py:210
  7.9 38.1 %collective-permute-start.2 = (bf16[4,256,256]{2,1,0:T(8,128)(2,1)S(1)}, bf16[4,256,256]{2,1,0:T(8,128)(2,1)S(1)}, u32[]{:S(2)}, u32[]{:S(2)}) collective-permute-start(bf16[4,256,256]{2,1,0:T(8,128)(2,1)S(1)} %get-tuple-element.25), channel_id=1, source_target_pairs={{0,128},{8,136},{16,144},{24,152},{32,160},{40,168},{48,176},{56,1... | collective-permute-start | bytes 1572872 | tf_op jit(solution)/shard_map/ppermute | solution.py:210
  10.5 32.7 %copy-start.1 = (bf16[1,256,1024]{2,1,0:T(8,128)(2,1)S(1)}, bf16[1,256,1024]{2,1,0:T(8,128)(2,1)}, u32[]{:S(2)}) copy-start(bf16[1,256,1024]{2,1,0:T(8,128)(2,1)} %param.8) | copy-start | bytes 1572868
  10.6 25.9 %collective-permute-start.9 = (bf16[2,256,256]{2,1,0:T(8,128)(2,1)S(1)}, bf16[2,256,256]{2,1,0:T(8,128)(2,1)S(1)}, u32[]{:S(2)}, u32[]{:S(2)}) collective-permute-start(bf16[2,256,256]{2,1,0:T(8,128)(2,1)S(1)} %get-tuple-element.33), channel_id=1, source_target_pairs={{0,64},{8,72},{16,80},{24,88},{32,96},{40,104},{48,112},{56,120},{... | collective-permute-start | bytes 786440 | tf_op jit(solution)/shard_map/ppermute | solution.py:210
  12.9 45.2 %collective-permute-start.4 = (bf16[4,256,256]{2,1,0:T(8,128)(2,1)}, bf16[4,256,256]{2,1,0:T(8,128)(2,1)}, u32[]{:S(2)}, u32[]{:S(2)}) collective-permute-start(bf16[4,256,256]{2,1,0:T(8,128)(2,1)} %get-tuple-element.27), channel_id=1, source_target_pairs={{0,24},{8,32},{16,40},{24,48},{32,56},{40,0},{48,8},{56,16},{64,88... | collective-permute-start | bytes 1572872 | tf_op jit(solution)/shard_map/ppermute | solution.py:210
  36.5 40.7 %collective-permute-start.5 = (bf16[4,256,256]{2,1,0:T(8,128)(2,1)}, bf16[4,256,256]{2,1,0:T(8,128)(2,1)}, u32[]{:S(2)}, u32[]{:S(2)}) collective-permute-start(bf16[4,256,256]{2,1,0:T(8,128)(2,1)} %get-tuple-element.28), channel_id=1, source_target_pairs={{0,40},{8,48},{16,56},{24,0},{32,8},{40,16},{48,24},{56,32},{64,10... | collective-permute-start | bytes 1572872 | tf_op jit(solution)/shard_map/ppermute | solution.py:210
  43.2 38.6 %collective-permute-start.13 = (bf16[256,1024]{1,0:T(8,128)(2,1)S(1)}, bf16[256,1024]{1,0:T(8,128)(2,1)S(1)}, u32[]{:S(2)}, u32[]{:S(2)}) collective-permute-start(bf16[256,1024]{1,0:T(8,128)(2,1)S(1)} %bitcast.17), channel_id=1, source_target_pairs={{0,8},{8,16},{16,24},{24,32},{32,40},{40,48},{48,56},{56,0},{64,72... | collective-permute-start | bytes 1572872 | tf_op jit(solution)/shard_map/ppermute | solution.py:210
  44.3 9.2 %collective-permute-start.10 = (bf16[2,256,256]{2,1,0:T(8,128)(2,1)S(1)}, bf16[2,256,256]{2,1,0:T(8,128)(2,1)S(1)}, u32[]{:S(2)}, u32[]{:S(2)}) collective-permute-start(bf16[2,256,256]{2,1,0:T(8,128)(2,1)S(1)} %get-tuple-element.34), channel_id=1, source_target_pairs={{0,192},{8,200},{16,208},{24,216},{32,224},{40,232},{48,240},{56,2... | collective-permute-start | bytes 786440 | tf_op jit(solution)/shard_map/ppermute | solution.py:210
  46.1 9.6 %collective-permute-start.11 = (bf16[2,256,256]{2,1,0:T(8,128)(2,1)S(1)}, bf16[2,256,256]{2,1,0:T(8,128)(2,1)S(1)}, u32[]{:S(2)}, u32[]{:S(2)}) collective-permute-start(bf16[2,256,256]{2,1,0:T(8,128)(2,1)S(1)} %get-tuple-element.35), channel_id=1, source_target_pairs={{0,128},{8,136},{16,144},{24,152},{32,160},{40,168},{48,176},{56,1... | collective-permute-start | bytes 786440 | tf_op jit(solution)/shard_map/ppermute | solution.py:210
  46.7 35.8 %copy-start.9 = (pred[32]{0:T(512)(128)(4,1)S(1)}, pred[32]{0:T(512)(128)(4,1)}, u32[]{:S(2)}) copy-start(pred[32]{0:T(512)(128)(4,1)} %constant.48) | copy-start | bytes 100
  46.7 35.9 %copy-start.7 = (s32[32]{0:T(128)S(1)}, s32[32]{0:T(128)}, u32[]{:S(2)}) copy-start(s32[32]{0:T(128)} %param.13) | copy-start | bytes 388
  46.7 36.6 %copy-start.8 = (pred[32,1]{0,1:T(4,128)(4,1)S(1)}, pred[32,1]{0,1:T(4,128)(4,1)}, u32[]{:S(2)}) copy-start(pred[32,1]{0,1:T(4,128)(4,1)} %constant.47) | copy-start | bytes 100
  47.6 9.0 %copy-start.3 = (bf16[4,256,256]{2,1,0:T(8,128)(2,1)}, bf16[4,256,256]{2,1,0:T(8,128)(2,1)S(1)}, u32[]{:S(2)}) copy-start(bf16[4,256,256]{2,1,0:T(8,128)(2,1)S(1)} %get-tuple-element.26) | copy-start | bytes 1572868
  53.4 46.1 %collective-permute-start.14 = (bf16[4,256,256]{2,1,0:T(8,128)(2,1)}, bf16[4,256,256]{2,1,0:T(8,128)(2,1)}, u32[]{:S(2)}, u32[]{:S(2)}) collective-permute-start(bf16[4,256,256]{2,1,0:T(8,128)(2,1)} %get-tuple-element.37), channel_id=1, source_target_pairs={{0,56},{8,0},{16,8},{24,16},{32,24},{40,32},{48,40},{56,48},{64,12... | collective-permute-start | bytes 1572872 | tf_op jit(solution)/shard_map/ppermute | solution.py:210
  56.5 0.8 copy-start.5
  57.3 54.4 %collective-permute-start.15 = (bf16[4,256,256]{2,1,0:T(8,128)(2,1)}, bf16[4,256,256]{2,1,0:T(8,128)(2,1)}, u32[]{:S(2)}, u32[]{:S(2)}) collective-permute-start(bf16[4,256,256]{2,1,0:T(8,128)(2,1)} %get-tuple-element.38), channel_id=1, source_target_pairs={{0,48},{8,56},{16,0},{24,8},{32,16},{40,24},{48,32},{56,40},{64,11... | collective-permute-start | bytes 1572872 | tf_op jit(solution)/shard_map/ppermute | solution.py:210
  78.5 28.1 %collective-permute-start.6 = (bf16[2,256,256]{2,1,0:T(8,128)(2,1)S(1)}, bf16[2,256,256]{2,1,0:T(8,128)(2,1)S(1)}, u32[]{:S(2)}, u32[]{:S(2)}) collective-permute-start(bf16[2,256,256]{2,1,0:T(8,128)(2,1)S(1)} %get-tuple-element.29), channel_id=1, source_target_pairs={{0,64},{8,72},{16,80},{24,88},{32,96},{40,104},{48,112},{56,120},{... | collective-permute-start | bytes 786440 | tf_op jit(solution)/shard_map/ppermute | solution.py:210
  78.8 27.7 %collective-permute-start.7 = (bf16[2,256,256]{2,1,0:T(8,128)(2,1)S(1)}, bf16[2,256,256]{2,1,0:T(8,128)(2,1)S(1)}, u32[]{:S(2)}, u32[]{:S(2)}) collective-permute-start(bf16[2,256,256]{2,1,0:T(8,128)(2,1)S(1)} %get-tuple-element.30), channel_id=1, source_target_pairs={{0,192},{8,200},{16,208},{24,216},{32,224},{40,232},{48,240},{56,2... | collective-permute-start | bytes 786440 | tf_op jit(solution)/shard_map/ppermute | solution.py:210
  81.8 24.8 %collective-permute-start.8 = (bf16[2,256,256]{2,1,0:T(8,128)(2,1)S(1)}, bf16[2,256,256]{2,1,0:T(8,128)(2,1)S(1)}, u32[]{:S(2)}, u32[]{:S(2)}) collective-permute-start(bf16[2,256,256]{2,1,0:T(8,128)(2,1)S(1)} %get-tuple-element.31), channel_id=1, source_target_pairs={{0,128},{8,136},{16,144},{24,152},{32,160},{40,168},{48,176},{56,1... | collective-permute-start | bytes 786440 | tf_op jit(solution)/shard_map/ppermute | solution.py:210
  111.7 9.2 %copy-start.4 = (bf16[4,256,256]{2,1,0:T(8,128)(2,1)S(1)}, bf16[4,256,256]{2,1,0:T(8,128)(2,1)}, u32[]{:S(2)}) copy-start(bf16[4,256,256]{2,1,0:T(8,128)(2,1)} %copy-done.3) | copy-start | bytes 1572868
  111.7 9.2 %copy-start.6 = (bf16[4,256,256]{2,1,0:T(8,128)(2,1)S(1)}, bf16[4,256,256]{2,1,0:T(8,128)(2,1)}, u32[]{:S(2)}) copy-start(bf16[4,256,256]{2,1,0:T(8,128)(2,1)} %copy-done.5) | copy-start | bytes 1572868
  111.7 9.3 %copy-start.2 = (bf16[1,256,256]{2,1,0:T(8,128)(2,1)S(1)}, bf16[1,256,256]{2,1,0:T(8,128)(2,1)}, u32[]{:S(2)}) copy-start(bf16[1,256,256]{2,1,0:T(8,128)(2,1)} %param.9) | copy-start | bytes 393220
  117.0 43.7 %collective-permute-start.16 = (bf16[256,1152]{1,0:T(8,128)(2,1)S(1)}, bf16[256,1152]{1,0:T(8,128)(2,1)S(1)}, u32[]{:S(2)}, u32[]{:S(2)}) collective-permute-start(bf16[256,1152]{1,0:T(8,128)(2,1)S(1)} %shard_map.94), channel_id=1, source_target_pairs={{0,56},{8,0},{16,8},{24,16},{32,24},{40,32},{48,40},{56,48},{64,12... | collective-permute-start | bytes 1769480 | tf_op jit(solution)/shard_map/ppermute | solution.py:210
  120.9 21.4 %collective-permute-start.3 = (bf16[4,256,256]{2,1,0:T(8,128)(2,1)S(1)}, bf16[4,256,256]{2,1,0:T(8,128)(2,1)S(1)}, u32[]{:S(2)}, u32[]{:S(2)}) collective-permute-start(bf16[4,256,256]{2,1,0:T(8,128)(2,1)S(1)} %copy-done.4), channel_id=1, source_target_pairs={{0,8},{8,16},{16,24},{24,32},{32,40},{40,48},{48,56},{56,0},{64,72... | collective-permute-start | bytes 1572872 | tf_op jit(solution)/shard_map/ppermute | solution.py:210
  120.9 34.9 %collective-permute-start.12 = (bf16[4,256,256]{2,1,0:T(8,128)(2,1)S(1)}, bf16[4,256,256]{2,1,0:T(8,128)(2,1)S(1)}, u32[]{:S(2)}, u32[]{:S(2)}) collective-permute-start(bf16[4,256,256]{2,1,0:T(8,128)(2,1)S(1)} %copy-done.6), channel_id=1, source_target_pairs={{0,16},{8,24},{16,32},{24,40},{32,48},{40,56},{48,0},{56,8},{64,80... | collective-permute-start | bytes 1572872 | tf_op jit(solution)/shard_map/ppermute | solution.py:210
